TPU v7x, 32 devices: a whole 2x2x4 slice. The times are simulated.
32 devices in a mesh: grp: 4 (over x, core), rep: 8 (over z, y).
Axes of the slice: x: 2, y: 2, z: 4, core: 2. Of those that a mesh axis runs over, the one named last changes fastest.
Arguments:
- tokens: bfloat16 [128, 1024, 576], P(('grp', 'rep')), may hold values from -6 to 6
- attention_gain: bfloat16 [576], replicated, may hold values from 0.099609375 to 1.8984375
- query_weight: bfloat16 [576, 576], replicated, may hold values from -0.25 to 0.25
- key_weight: bfloat16 [576, 192], replicated, may hold values from -0.25 to 0.25
- value_weight: bfloat16 [576, 192], replicated, may hold values from -0.25 to 0.25
- output_weight: bfloat16 [576, 576], replicated, may hold values from -0.75 to 0.75
- feed_gain: bfloat16 [576], replicated, may hold values from 0.099609375 to 1.8984375
- gate_weight: bfloat16 [576, 1536], replicated, may hold values from -0.25 to 0.25
- up_weight: bfloat16 [576, 1536], replicated, may hold values from -0.25 to 0.25
- down_weight: bfloat16 [1536, 576], replicated, may hold values from -0.21875 to 0.21875
- router: bfloat16 [3, 576], replicated, may hold values from -0.1875 to 0.1875
- out_grad: bfloat16 [128, 1024, 576], P(('grp', 'rep')), may hold values from -6 to 6
- doc_lengths: int32 [4, 32, 4], P(None, 'rep'), may hold values from 1 to 512, 1024 in all within a row
- picks_first: int32 [4, 32, 192], P(None, 'rep'), may hold values from 0 to 1023, as said below
- picks_second: int32 [4, 32, 96], P(None, 'rep'), may hold values from 0 to 1023, as said below
- picks_third: int32 [4, 32, 48], P(None, 'rep'), may hold values from 0 to 1023, as said below
- routes: int32 [4, 32, 3, 2], P(None, 'rep'), may hold values from 0 to 192, as said below
Outputs:
- out_state: bfloat16 [128, 1024, 576], P(('grp', 'rep'))
- grad_tokens: bfloat16 [128, 1024, 576], P(('grp', 'rep'))
- grad_attention_gain: float32 [576], replicated
- grad_query_weight: float32 [576, 576], replicated
- grad_key_weight: float32 [576, 192], replicated
- grad_value_weight: float32 [576, 192], replicated
- grad_output_weight: float32 [576, 576], replicated
- grad_feed_gain: float32 [576], replicated
- grad_gate_weight: float32 [576, 1536], replicated
- grad_up_weight: float32 [576, 1536], replicated
- grad_down_weight: float32 [1536, 576], replicated
- grad_router: float32 [3, 576], replicated
Inputs may be any that keep to these rules, and one draw needn't show every extreme that they name: routes[i, c, r, 0] is the count of picked tokens of that sequence at recursion r + 1: from 64 to 192 at the first, 32 to 96 at the second, 16 to 48 at the third, never rising from one recursion to the next, each largest count present in every draw. routes[i, c, r, 1] is the sequence's bucket, a grp index; the sequences of one device go to different buckets, and every bucket receives exactly 512, 256, 128 picked tokens at recursions 1, 2, 3. `picks_first`: the first count entries of a row are distinct positions in rising order, the rest 0; a recursion's picked tokens are among the previous recursion's. `picks_second`: as picks_first, for recursion 2. `picks_third`: as picks_first, for recursion 3. `doc_lengths`: each row sums to 1024.
All inputs are finite; a program needn't handle non-finite values.
Results may differ from a plain program's by a relative error of at most 0.03.
Values may be sent and summed in bfloat16 or wider, within the bound.
A program may use at most 448 MiB of HBM per device.

v0:
```python
import jax
import jax.numpy as jnp
from jax import lax
from jax.sharding import PartitionSpec as P

HEAD_DIM = 64
NREC = 3


EPSILON = 1e-05
ROPE_BASE = 10000.0
SCORE_SCALE = 0.125
MASKED = -1e30


def rms_scale(values):
    return lax.rsqrt(jnp.mean(values * values, axis=-1, keepdims=True) + EPSILON)


def exact_parts(values):
    upper = values.astype(jnp.bfloat16)
    rest = values - upper.astype(jnp.float32)
    middle_part = rest.astype(jnp.bfloat16)
    lowest = (rest - middle_part.astype(jnp.float32)).astype(jnp.bfloat16)
    return (upper, middle_part, lowest)


def pick_rows(whole, selector):
    parts = exact_parts(whole)
    taken = [
        jnp.einsum("sjp,spd->sjd", selector, piece, preferred_element_type=jnp.float32)
        for piece in parts
    ]
    return taken[0] + taken[1] + taken[2]


def place_rows(whole, selector, added):
    parts = exact_parts(added)
    spread = [
        jnp.einsum("sjp,sjd->spd", selector, piece, preferred_element_type=jnp.float32)
        for piece in parts
    ]
    return whole + (spread[0] + spread[1] + spread[2])


def rope_tables(positions):
    halfway = HEAD_DIM // 2
    inverse = ROPE_BASE ** (-(jnp.arange(halfway, dtype=jnp.float32) * (2.0 / HEAD_DIM)))
    angles = positions.astype(jnp.float32)[..., None] * inverse
    cosines = jnp.cos(angles)
    sine_values = jnp.sin(angles)
    return (
        jnp.concatenate([cosines, cosines], -1),
        jnp.concatenate([sine_values, sine_values], -1),
    )


def rotate(values, cosines, sine_values):
    halfway = values.shape[-1] // 2
    turned = jnp.concatenate([-values[..., halfway:], values[..., :halfway]], -1)
    return values * cosines + turned * sine_values


def unrotate(grads_in, cosines, sine_values):
    halfway = grads_in.shape[-1] // 2
    scaled = grads_in * sine_values
    return grads_in * cosines + jnp.concatenate([scaled[..., halfway:], -scaled[..., :halfway]], -1)


def attention_mask(labels, starts, positions, active):
    same_doc = (labels[:, :, None] == labels[:, None, :]) & (
        starts[:, :, None] == starts[:, None, :]
    )
    causal = positions[:, None, :] <= positions[:, :, None]
    length = labels.shape[1]
    return same_doc & causal & active[:, None, :] | jnp.eye(length, dtype=bool)[None]


def block_inner(rows_low, allowed, positions, weights, kept_lse):
    (
        attention_gain,
        query_weight,
        key_weight,
        value_weight,
        output_weight,
        feed_gain,
        gate_weight,
        up_weight,
        down_weight,
    ) = weights
    group_count, length, model_width = rows_low.shape
    kv_count = key_weight.shape[1] // HEAD_DIM
    per_group = query_weight.shape[1] // key_weight.shape[1]
    flat_rows = rows_low.reshape(group_count * length, model_width).astype(jnp.float32)
    inverse_one = rms_scale(flat_rows)
    normed_one = (flat_rows * inverse_one * attention_gain).astype(jnp.bfloat16)
    query_rows = jnp.dot(normed_one, query_weight, preferred_element_type=jnp.float32)
    key_pre = jnp.dot(normed_one, key_weight, preferred_element_type=jnp.float32)
    value_low = jnp.dot(normed_one, value_weight, preferred_element_type=jnp.float32).astype(
        jnp.bfloat16
    )
    cosines, sine_values = rope_tables(positions)
    query_low = rotate(
        query_rows.reshape(group_count, length, kv_count, per_group, HEAD_DIM),
        cosines[:, :, None, None],
        sine_values[:, :, None, None],
    ).astype(jnp.bfloat16)
    key_low = rotate(
        key_pre.reshape(group_count, length, kv_count, HEAD_DIM),
        cosines[:, :, None],
        sine_values[:, :, None],
    ).astype(jnp.bfloat16)
    value_low = value_low.reshape(group_count, length, kv_count, HEAD_DIM)
    scores = (
        jnp.einsum("gqkhd,gskd->gkhqs", query_low, key_low, preferred_element_type=jnp.float32)
        * SCORE_SCALE
    )
    scores = jnp.where(allowed[:, None, None], scores, MASKED)
    if kept_lse is None:
        highest = jnp.max(scores, axis=-1, keepdims=True)
        kept_lse = highest + jnp.log(jnp.sum(jnp.exp(scores - highest), axis=-1, keepdims=True))
    shares = jnp.exp(scores - kept_lse)
    shares_low = shares.astype(jnp.bfloat16)
    mixed_rows = jnp.einsum(
        "gkhqs,gskd->gqkhd", shares_low, value_low, preferred_element_type=jnp.float32
    )
    mixed_low = mixed_rows.reshape(group_count * length, model_width).astype(jnp.bfloat16)
    attended = jnp.dot(mixed_low, output_weight, preferred_element_type=jnp.float32)
    middle = flat_rows + attended
    inverse_two = rms_scale(middle)
    normed_two = (middle * inverse_two * feed_gain).astype(jnp.bfloat16)
    gate_pre = jnp.dot(normed_two, gate_weight, preferred_element_type=jnp.float32)
    up_pre = jnp.dot(normed_two, up_weight, preferred_element_type=jnp.float32)
    hidden = (jax.nn.silu(gate_pre) * up_pre).astype(jnp.bfloat16)
    return (
        flat_rows,
        inverse_one,
        normed_one,
        query_low,
        key_low,
        value_low,
        cosines,
        sine_values,
        shares,
        shares_low,
        mixed_low,
        attended,
        middle,
        inverse_two,
        normed_two,
        gate_pre,
        up_pre,
        hidden,
        kept_lse,
    )


def block_forward(rows_low, allowed, positions, weights):
    inner = block_inner(rows_low, allowed, positions, weights, None)
    attended = inner[11]
    hidden = inner[17]
    change = attended + jnp.dot(hidden, weights[8], preferred_element_type=jnp.float32)
    return (change, inner[18])


def block_backward(rows_low, allowed, positions, kept_lse, change_grad, weights):
    (
        attention_gain,
        query_weight,
        key_weight,
        value_weight,
        output_weight,
        feed_gain,
        gate_weight,
        up_weight,
        down_weight,
    ) = weights
    (
        flat_rows,
        inverse_one,
        normed_one,
        query_low,
        key_low,
        value_low,
        cosines,
        sine_values,
        shares,
        shares_low,
        mixed_low,
        attended,
        middle,
        inverse_two,
        normed_two,
        gate_pre,
        up_pre,
        hidden,
        kept_lse,
    ) = block_inner(rows_low, allowed, positions, weights, kept_lse)
    group_count, length, model_width = rows_low.shape
    kv_count = key_weight.shape[1] // HEAD_DIM
    per_group = query_weight.shape[1] // key_weight.shape[1]
    change_flat = change_grad.reshape(group_count * length, model_width)
    grad_down = jnp.einsum("rf,rd->fd", hidden, change_flat, preferred_element_type=jnp.float32)
    hidden_grad = jnp.einsum(
        "rd,fd->rf", change_flat, down_weight, preferred_element_type=jnp.float32
    )
    gate_sigmoid = jax.nn.sigmoid(gate_pre)
    gate_grad = (
        hidden_grad * up_pre * (gate_sigmoid + gate_pre * gate_sigmoid * (1.0 - gate_sigmoid))
    ).astype(jnp.bfloat16)
    up_grad = (hidden_grad * gate_pre * gate_sigmoid).astype(jnp.bfloat16)
    grad_gate = jnp.einsum("rd,rf->df", normed_two, gate_grad, preferred_element_type=jnp.float32)
    grad_up = jnp.einsum("rd,rf->df", normed_two, up_grad, preferred_element_type=jnp.float32)
    normed_two_grad = jnp.einsum(
        "rf,df->rd", gate_grad, gate_weight, preferred_element_type=jnp.float32
    ) + jnp.einsum("rf,df->rd", up_grad, up_weight, preferred_element_type=jnp.float32)
    scaled_two = middle * inverse_two
    grad_feed_gain = jnp.sum(normed_two_grad * scaled_two, axis=0)
    upstream_two = normed_two_grad * feed_gain
    middle_grad = inverse_two * (
        upstream_two - scaled_two * jnp.mean(upstream_two * scaled_two, axis=-1, keepdims=True)
    )
    attended_grad = (change_flat.astype(jnp.float32) + middle_grad).astype(jnp.bfloat16)
    grad_output = jnp.einsum(
        "rc,rd->cd", mixed_low, attended_grad, preferred_element_type=jnp.float32
    )
    mixed_grad = jnp.einsum(
        "rd,cd->rc", attended_grad, output_weight, preferred_element_type=jnp.float32
    ).astype(jnp.bfloat16)
    mixed_grad = mixed_grad.reshape(group_count, length, kv_count, per_group, HEAD_DIM)
    prob_grad = jnp.einsum(
        "gqkhd,gskd->gkhqs", mixed_grad, value_low, preferred_element_type=jnp.float32
    )
    value_sum = jnp.einsum(
        "gkhqs,gqkhd->gskd", shares_low, mixed_grad, preferred_element_type=jnp.float32
    )
    score_grad = (
        shares * (prob_grad - jnp.sum(shares * prob_grad, axis=-1, keepdims=True))
    ).astype(jnp.bfloat16)
    query_back = (
        jnp.einsum("gkhqs,gskd->gqkhd", score_grad, key_low, preferred_element_type=jnp.float32)
        * SCORE_SCALE
    )
    key_back = (
        jnp.einsum("gkhqs,gqkhd->gskd", score_grad, query_low, preferred_element_type=jnp.float32)
        * SCORE_SCALE
    )
    query_grad = (
        unrotate(query_back, cosines[:, :, None, None], sine_values[:, :, None, None])
        .astype(jnp.bfloat16)
        .reshape(group_count * length, model_width)
    )
    key_grad = (
        unrotate(key_back, cosines[:, :, None], sine_values[:, :, None])
        .astype(jnp.bfloat16)
        .reshape(group_count * length, kv_count * HEAD_DIM)
    )
    value_grad = value_sum.astype(jnp.bfloat16).reshape(group_count * length, kv_count * HEAD_DIM)
    grad_query = jnp.einsum("rd,rc->dc", normed_one, query_grad, preferred_element_type=jnp.float32)
    grad_key = jnp.einsum("rd,rc->dc", normed_one, key_grad, preferred_element_type=jnp.float32)
    grad_value = jnp.einsum("rd,rc->dc", normed_one, value_grad, preferred_element_type=jnp.float32)
    normed_one_grad = (
        jnp.einsum("rc,dc->rd", query_grad, query_weight, preferred_element_type=jnp.float32)
        + jnp.einsum("rc,dc->rd", key_grad, key_weight, preferred_element_type=jnp.float32)
        + jnp.einsum("rc,dc->rd", value_grad, value_weight, preferred_element_type=jnp.float32)
    )
    scaled_one = flat_rows * inverse_one
    grad_attention_gain = jnp.sum(normed_one_grad * scaled_one, axis=0)
    upstream_one = normed_one_grad * attention_gain
    rows_grad = middle_grad + inverse_one * (
        upstream_one - scaled_one * jnp.mean(upstream_one * scaled_one, axis=-1, keepdims=True)
    )
    return (
        rows_grad,
        (
            grad_attention_gain,
            grad_query,
            grad_key,
            grad_value,
            grad_output,
            grad_feed_gain,
            grad_gate,
            grad_up,
            grad_down,
        ),
    )


def per_device(
    tokens,
    attention_gain,
    query_weight,
    key_weight,
    value_weight,
    output_weight,
    feed_gain,
    gate_weight,
    up_weight,
    down_weight,
    router,
    out_grad,
    doc_lengths,
    picks_first,
    picks_second,
    picks_third,
    routes,
):
    seq_count, seq_len, model_width = tokens.shape
    bucket_count = lax.axis_size("grp")
    own_bucket = lax.axis_index("grp")
    weights = (
        attention_gain.astype(jnp.float32),
        query_weight,
        key_weight,
        value_weight,
        output_weight,
        feed_gain.astype(jnp.float32),
        gate_weight,
        up_weight,
        down_weight,
    )
    router_rows = router.astype(jnp.float32)
    doc_ends = jnp.cumsum(doc_lengths, axis=-1)
    source_ids = jnp.arange(bucket_count)
    seq_positions = jnp.arange(seq_len, dtype=jnp.int32)
    residual = tokens.astype(jnp.float32)
    stored = []
    for recursion, pick_table in enumerate((picks_first, picks_second, picks_third)):
        slot_count = pick_table.shape[-1]
        count_table = routes[:, :, recursion, 0]
        target_table = routes[:, :, recursion, 1]
        start_table = jnp.sum(
            jnp.where(
                doc_ends[:, :, None, :] <= pick_table[..., None], doc_lengths[:, :, None, :], 0
            ),
            axis=-1,
        )
        pick_list = jnp.take(pick_table, own_bucket, axis=0)
        count_list = jnp.take(count_table, own_bucket, axis=0)
        target_list = jnp.take(target_table, own_bucket, axis=0)
        active = jnp.arange(slot_count)[None, :] < count_list[:, None]
        selector = (pick_list[:, :, None] == seq_positions[None, None, :]).astype(jnp.bfloat16)
        picked_rows = pick_rows(residual, selector)
        gate_values = jax.nn.sigmoid(jnp.sum(picked_rows * router_rows[recursion], axis=-1))
        rows_low = picked_rows.astype(jnp.bfloat16)
        hit_mask = target_list[None, :] == source_ids[:, None]
        hit_low = hit_mask.astype(jnp.bfloat16)
        live_rows = jnp.where(active[..., None], rows_low, jnp.zeros((), jnp.bfloat16))
        outgoing = jnp.einsum(
            "bs,sjd->bjd", hit_low, live_rows, preferred_element_type=jnp.float32
        ).astype(jnp.bfloat16)
        incoming = lax.all_to_all(outgoing, "grp", split_axis=0, concat_axis=0, tiled=True)
        arriving = target_table == own_bucket
        arrived = jnp.sum(jnp.where(arriving, count_table, 0), axis=1)
        source_positions = jnp.sum(jnp.where(arriving[..., None], pick_table, 0), axis=1)
        source_starts = jnp.sum(jnp.where(arriving[..., None], start_table, 0), axis=1)
        finish = jnp.cumsum(arrived)
        first_row = finish - arrived
        capacity = 2 * (slot_count // 3) * seq_count
        compact_at = jnp.arange(capacity)
        source = jnp.sum((finish[None, :] <= compact_at[:, None]).astype(jnp.int32), axis=1)
        source_first = jnp.sum(
            jnp.where(source_ids[None, :] == source[:, None], first_row[None, :], 0), axis=1
        )
        flat_index = source * slot_count + compact_at - source_first
        packed = jnp.take(
            incoming.reshape(bucket_count * slot_count, model_width), flat_index, axis=0
        )[None]
        positions = jnp.take(source_positions.reshape(-1), flat_index)[None]
        doc_start = jnp.take(source_starts.reshape(-1), flat_index)[None]
        allowed = attention_mask(
            source[None], doc_start, positions, jnp.ones((1, capacity), dtype=bool)
        )
        change, log_total = block_forward(packed, allowed, positions, weights)
        slot_index = jnp.clip(first_row[:, None] + jnp.arange(slot_count)[None, :], 0, capacity - 1)
        slot_live = jnp.arange(slot_count)[None, :] < arrived[:, None]
        change_slots = jnp.take(
            change.astype(jnp.bfloat16), slot_index.reshape(-1), axis=0
        ).reshape(bucket_count, slot_count, model_width)
        returned = jnp.where(slot_live[..., None], change_slots, jnp.zeros((), jnp.bfloat16))
        coming_back = lax.all_to_all(returned, "grp", split_axis=0, concat_axis=0, tiled=True)
        change_rows = jnp.einsum(
            "bs,bjd->sjd", hit_low, coming_back, preferred_element_type=jnp.float32
        )
        stored.append(
            (
                selector,
                active,
                picked_rows,
                gate_values,
                change_rows,
                hit_low,
                packed,
                allowed,
                positions,
                log_total,
                flat_index,
                slot_index,
                slot_live,
            )
        )
        update = gate_values[..., None] * change_rows * active[..., None].astype(jnp.float32)
        residual = place_rows(residual, selector, update)
    grad_totals = tuple((jnp.zeros(weight_item.shape, jnp.float32) for weight_item in weights))
    router_terms = [None] * NREC
    residual_grad = out_grad.astype(jnp.float32)
    for recursion in (2, 1, 0):
        (
            selector,
            active,
            picked_rows,
            gate_values,
            change_rows,
            hit_low,
            packed,
            allowed,
            positions,
            log_total,
            flat_index,
            slot_index,
            slot_live,
        ) = stored[recursion]
        slot_count = selector.shape[1]
        active_float = active.astype(jnp.float32)
        row_grad = pick_rows(residual_grad, selector)
        change_grad = (gate_values[..., None] * row_grad * active_float[..., None]).astype(
            jnp.bfloat16
        )
        logit_grad = (
            jnp.sum(row_grad * change_rows, axis=-1)
            * active_float
            * gate_values
            * (1.0 - gate_values)
        )
        router_terms[recursion] = jnp.sum(logit_grad[..., None] * picked_rows, axis=(0, 1))
        outgoing_grad = jnp.einsum(
            "bs,sjd->bjd", hit_low, change_grad, preferred_element_type=jnp.float32
        ).astype(jnp.bfloat16)
        incoming_grad = lax.all_to_all(
            outgoing_grad, "grp", split_axis=0, concat_axis=0, tiled=True
        )
        packed_grad = jnp.take(
            incoming_grad.reshape(bucket_count * slot_count, model_width), flat_index, axis=0
        )[None]
        rows_grad, grad_terms = block_backward(
            packed, allowed, positions, log_total, packed_grad, weights
        )
        grad_slots = jnp.take(
            rows_grad.astype(jnp.bfloat16), slot_index.reshape(-1), axis=0
        ).reshape(bucket_count, slot_count, model_width)
        back_slots = jnp.where(slot_live[..., None], grad_slots, jnp.zeros((), jnp.bfloat16))
        coming_grad = lax.all_to_all(back_slots, "grp", split_axis=0, concat_axis=0, tiled=True)
        sent_grad = jnp.einsum(
            "bs,bjd->sjd", hit_low, coming_grad, preferred_element_type=jnp.float32
        )
        grad_totals = tuple(
            (running + fresh_term for running, fresh_term in zip(grad_totals, grad_terms))
        )
        total_grad = (logit_grad[..., None] * router_rows[recursion] + sent_grad) * active_float[
            ..., None
        ]
        residual_grad = place_rows(residual_grad, selector, total_grad)
    router_grad = jnp.stack(router_terms, 0)
    (
        gain_one_total,
        query_total,
        key_total,
        value_total,
        output_total,
        gain_two_total,
        gate_total,
        up_total,
        down_total,
    ) = grad_totals
    (
        gain_one_sum,
        query_sum,
        key_sum,
        value_sum,
        output_sum,
        gain_two_sum,
        gate_sum,
        up_sum,
        down_sum,
        router_sum,
    ) = lax.psum(
        (
            gain_one_total,
            query_total,
            key_total,
            value_total,
            output_total,
            gain_two_total,
            gate_total,
            up_total,
            down_total,
            router_grad,
        ),
        ("grp", "rep"),
    )
    return (
        residual.astype(jnp.bfloat16),
        residual_grad.astype(jnp.bfloat16),
        gain_one_sum,
        query_sum,
        key_sum,
        value_sum,
        output_sum,
        gain_two_sum,
        gate_sum,
        up_sum,
        down_sum,
        router_sum,
    )


def solution(mesh):
    placed = (
        P(("grp", "rep"), None, None),
        P(),
        P(),
        P(),
        P(),
        P(),
        P(),
        P(),
        P(),
        P(),
        P(),
        P(("grp", "rep"), None, None),
        P(None, "rep", None),
        P(None, "rep", None),
        P(None, "rep", None),
        P(None, "rep", None),
        P(None, "rep", None, None),
    )
    return jax.shard_map(
        per_device,
        mesh=mesh,
        in_specs=placed,
        out_specs=(
            P(("grp", "rep"), None, None),
            P(("grp", "rep"), None, None),
            P(),
            P(),
            P(),
            P(),
            P(),
            P(),
            P(),
            P(),
            P(),
            P(),
        ),
        check_vma=False,
    )
```

profile of v0, /device:TPU:1, one launch (start us, length us, event | category | flops | bytes accessed | tf_op | source)
XLA Modules:
  0.0 756.3 jit_solution(2094303545600792337)
XLA Ops:
  8.0 4.4 fusion.34
  20.0 4.3 all-to-all-start
  76.7 3.5 multiply_convert_fusion.2
  87.8 3.5 all-to-all-start.1
  93.3 4.6 fusion.36
  97.9 6.1 all-to-all-done.1
  104.9 4.8 fusion.50
  109.7 4.7 fusion.49
  114.5 9.2 %convert_add_fusion.1 = f32[4,1024,576]{1,2,0:T(8,128)S(1)} fusion(bf16[4,1024,576]{1,2,0:T(8,128)(2,1)} %param.37, f32[4,1024,576]{1,2,0:T(8,128)} %fusion.50, f32[4,1024,576]{1,2,0:T(8,128)} %fusion.49, s32[4,192]{1,0:T(4,128)S(1)} %select_bitcast_fusion, f32[4,192,576]{2,0,1:T(4,128)S(1)} %fusion.131, f32[4,192]{1,0:T(4,128)S(1)} %get-tuple-element.177, ...), kind=kOutput, calls=%fused_computation.20 | convolution fusion | flops 920174592 | bytes 34808832 | tf_op jit(solution)/shard_map/sjp,sjd->spd/dot_general | solution.py:40
  131.4 4.7 all-to-all-start.2
  136.1 4.6 fusion.42
  163.8 4.5 all-to-all-start.3
  169.8 6.2 all-to-all-done.3
  176.5 6.2 fusion.65
  182.6 5.2 fusion.64
  187.9 10.7 %add_add_fusion.1 = f32[4,1024,576]{1,2,0:T(8,128)} fusion(f32[4,1024,576]{1,2,0:T(8,128)S(1)} %bitcast.453, f32[4,1024,576]{1,2,0:T(8,128)} %fusion.65, f32[4,1024,576]{1,2,0:T(8,128)} %fusion.64, s32[4,96]{1,0:T(4,128)S(1)} %fusion.292, f32[4,96,576]{2,0,1:T(4,128)S(1)} %fusion.186, f32[4,96]{1,0:T(4,128)S(1)} %get-tuple-element.175, ...), kind=kOutput, calls=%fused_computation.43 | convolution fusion | flops 462446592 | bytes 38638080 | tf_op jit(solution)/shard_map/sjp,sjd->spd/dot_general | solution.py:40
  198.6 8.0 %fusion.40 = f32[4,48,576]{2,1,0:T(8,128)S(1)} fusion(f32[4,1024,576]{1,2,0:T(8,128)} %add_add_fusion.1, s32[4,48]{1,0:T(4,128)S(1)} %fusion.294), kind=kOutput, calls=%fused_computation.73 | convolution fusion | flops 243204096 | bytes 9880320 | tf_op jit(solution)/shard_map/sjp,spd->sjd/dot_general | solution.py:31
  211.9 4.2 all-to-all-start.4
  216.3 4.9 multiply_convert_fusion.14
  222.4 4.4 all-to-all-start.6
  264.0 3.5 all-to-all-start.5
  269.1 3.4 all-to-all-done.5
  272.5 4.4 all-to-all-start.7
  277.4 5.1 fusion.150
  284.6 5.2 fusion.147
  289.8 7.7 %convert_add_fusion = f32[4,1024,576]{1,2,0:T(8,128)S(1)} fusion(bf16[4,1024,576]{1,2,0:T(8,128)(2,1)} %param.48, f32[4,1024,576]{1,2,0:T(8,128)S(1)} %fusion.148, f32[4,1024,576]{1,2,0:T(8,128)} %fusion.147, s32[4,48]{1,0:T(4,128)S(1)} %copy-done.171, f32[4,48,576]{2,0,1:T(4,128)} %copy-done.61, f32[4,48]{1,0:T(4,128)S(1)} %subtract_multiply_fusion.5, ...), kind=kOutput, calls=%fused_computation.18 | convolution fusion | flops 237232128 | bytes 33477120 | tf_op jit(solution)/shard_map/sjp,sjd->spd/dot_general | solution.py:40
  304.6 3.7 all-to-all-start.8
  308.4 5.2 fusion.149
  342.5 5.4 all-to-all-start.9
  350.3 5.2 all-to-all-done.9
  357.1 5.1 fusion.63
  362.2 5.1 fusion.62
  367.3 10.2 %add_add_fusion = f32[4,1024,576]{1,2,0:T(8,128)S(1)} fusion(f32[4,1024,576]{1,2,0:T(8,128)} %copy-done.5, f32[4,1024,576]{1,2,0:T(8,128)} %fusion.63, f32[4,1024,576]{1,2,0:T(8,128)} %fusion.62, s32[4,96]{1,0:T(4,128)S(1)} %copy-done.167, f32[4,96,576]{2,0,1:T(4,128)S(1)} %fusion.182, f32[4,96]{1,0:T(4,128)S(1)} %subtract_multiply_fusion.4, ...), kind=kOutput, calls=%fused_computation.37 | convolution fusion | flops 462667776 | bytes 38640384 | tf_op jit(solution)/shard_map/sjp,sjd->spd/dot_general | solution.py:40
  382.2 3.3 multiply_reduce_fusion.1
  387.8 4.4 all-to-all-start.10
  392.2 3.6 fusion.384
  398.2 6.8 all-to-all-done.10
  407.6 5.5 multiply_convert_fusion
  423.8 5.6 fusion.6
  429.5 11.3 %fusion.33 = bf16[3,3,512,512]{2,3,1,0:T(8,128)(2,1)} fusion(f32[3,512,512,3]{2,1,3,0:T(8,128)} %get-tuple-element.218, f32[3,512,512,3]{2,1,3,0:T(8,128)} %copy-done.2, f32[3,3,512]{2,1,0:T(4,128)S(1)} %get-tuple-element.217, f32[3,3,512]{2,1,0:T(4,128)S(1)} %copy-done.169, pred[512,512]{0,1:T(8,128)(4,1)S(1)} %copy-done.20), kind=kLoop, calls=%fused_computation.68 | loop fusion | flops 14155776 | bytes 23891968 | tf_op jit(solution)/shard_map/reshape.198
  440.8 4.2 broadcast_multiply_fusion.2
  473.7 14.2 %add_convert_fusion.1 = bf16[4,1024,576]{1,2,0:T(8,128)(2,1)} fusion(f32[4,1024,576]{1,2,0:T(8,128)} %add_add_fusion.1, f32[4,1024,576]{1,2,0:T(8,128)} %fusion.150, f32[4,1024,576]{1,2,0:T(8,128)} %fusion.149, s32[4,48]{1,0:T(4,128)} %copy-done.170, f32[4,48,576]{2,0,1:T(4,128)} %copy-done.48, f32[4,48]{1,0:T(4,128)} %copy-done.185, f32[4,48]{1,0:T(4,128)} %copy-done.202), kind=kOutput, calls=%fused_computation.40 | convolution fusion | flops 237121536 | bytes 33474816 | tf_op jit(solution)/shard_map/sjp,sjd->spd/dot_general | solution.py:40
  498.6 4.4 all-to-all-start.11
  505.0 53.2 %all-reduce = (f32[576]{0:T(1024)}, f32[576]{0:T(1024)}, f32[3,576]{1,0:T(4,128)}) all-reduce(f32[576]{0:T(1024)S(1)} %add_add_fusion.10, f32[576]{0:T(1024)S(1)} %add_add_fusion.9, f32[3,576]{1,0:T(4,128)S(1)} %pad_maximum_fusion), channel_id=1, replica_groups=mesh['grp'=4,'rep'=8] {'grp','rep'}, use_global_device_ids=true, to_apply=%region_52.63 | all-reduce | flops 2880 | bytes 23040 | tf_op jit(solution)/shard_map/psum | solution.py:486
  559.2 5.7 fusion.48
  564.9 4.7 fusion.47
  569.6 10.8 %add_convert_fusion = bf16[4,1024,576]{1,2,0:T(8,128)(2,1)} fusion(f32[4,1024,576]{1,2,0:T(8,128)S(1)} %bitcast.457, f32[4,1024,576]{1,2,0:T(8,128)} %fusion.48, f32[4,1024,576]{1,2,0:T(8,128)} %fusion.47, s32[4,192]{1,0:T(4,128)S(1)} %select_bitcast_fusion, f32[4,192,576]{2,0,1:T(4,128)} %copy-done.10, f32[4,192]{1,0:T(4,128)S(1)} %copy-done.144, ...), kind=kOutput, calls=%fused_computation.34 | convolution fusion | flops 920616960 | bytes 34811136 | tf_op jit(solution)/shard_map/sjp,sjd->spd/dot_general | solution.py:40
  580.4 154.0 %all-reduce.4.cloned.1.call-done = (f32[576,576]{1,0:T(8,128)}, f32[576,192]{0,1:T(8,128)}, f32[576,192]{0,1:T(8,128)}, f32[576,576]{1,0:T(8,128)}, f32[576,1536...) async-done(((f32[576,576]{1,0:T(8,128)}, f32[576,192]{0,1:T(8,128)}, f32[576,192]{0,1:T(8,128)}, f32[576,576]{1,0:T(8,128)}, f32[576,1536]{1,0:T(8,128)}, ...) | async-done | bytes 14155792 | tf_op jit(solution)/shard_map/psum | solution.py:486
  (923 shorter events, 268.1 us)
Async XLA Ops:
  7.2 74.2 %copy-start = (bf16[1536,576]{0,1:T(8,128)(2,1)S(1)}, bf16[1536,576]{0,1:T(8,128)(2,1)}, u32[]{:S(2)}) copy-start(bf16[1536,576]{0,1:T(8,128)(2,1)} %param.46) | copy-start | bytes 5308420
  14.4 13.1 %copy-start.247 = (s32[4,4,1,1]{1,3,2,0:T(1,128)}, s32[4,4,1,1]{1,3,2,0:T(1,128)S(1)}, u32[]{:S(2)}) copy-start(s32[4,4,1,1]{1,3,2,0:T(1,128)S(1)} %get-tuple-element.156) | copy-start | bytes 196
  14.6 99.9 %copy-start.122 = (f32[4,192]{1,0:T(4,128)}, f32[4,192]{1,0:T(4,128)S(1)}, u32[]{:S(2)}) copy-start(f32[4,192]{1,0:T(4,128)S(1)} %get-tuple-element.177) | copy-start | bytes 9220
  20.0 38.3 %all-to-all-start = ((bf16[4,192,576]{2,1,0:T(8,128)(2,1)}), bf16[4,192,576]{2,1,0:T(8,128)(2,1)S(1)}, u32[]{:S(2)}, u32[]{:S(2)}) async-start(bf16[4,192,576]{2,1,0:T(8,128)(2,1)} %copy.196), calls=%async_computation | async-start | bytes 1966080 | tf_op jit(solution)/shard_map/all_to_all | solution.py:352
  26.8 161.0 %copy-start.166 = (s32[4,96]{1,0:T(4,128)}, s32[4,96]{1,0:T(4,128)S(1)}, u32[]{:S(2)}) copy-start(s32[4,96]{1,0:T(4,128)S(1)} %fusion.292) | copy-start | bytes 4612
  27.5 25.1 %copy-start.271 = (s32[4]{0:T(128)}, s32[4]{0:T(128)S(1)}, u32[]{:S(2)}) copy-start(s32[4]{0:T(128)S(1)} %get-tuple-element.228) | copy-start | bytes 52
  27.6 26.3 %copy-start.273 = (s32[4]{0:T(128)}, s32[4]{0:T(128)S(1)}, u32[]{:S(2)}) copy-start(s32[4]{0:T(128)S(1)} %get-tuple-element.229) | copy-start | bytes 52
  29.3 187.0 %copy-start.170 = (s32[4,48]{1,0:T(4,128)}, s32[4,48]{1,0:T(4,128)S(1)}, u32[]{:S(2)}) copy-start(s32[4,48]{1,0:T(4,128)S(1)} %fusion.294) | copy-start | bytes 2308
  38.8 109.2 %copy-start.206 = (pred[256]{0:T(512)(128)(4,1)}, pred[256]{0:T(512)(128)(4,1)S(1)}, u32[]{:S(2)}) copy-start(pred[256]{0:T(512)(128)(4,1)S(1)} %get-tuple-element.108) | copy-start | bytes 772
  43.7 14.6 %copy-start.219 = (s32[1024]{0:T(1024)}, s32[1024]{0:T(1024)S(1)}, u32[]{:S(2)}) copy-start(s32[1024]{0:T(1024)S(1)} %pad_clamp_fusion.5) | copy-start | bytes 12292
  46.2 26.7 %copy-start.209 = (pred[512]{0:T(512)(128)(4,1)}, pred[512]{0:T(512)(128)(4,1)S(1)}, u32[]{:S(2)}) copy-start(pred[512]{0:T(512)(128)(4,1)S(1)} %get-tuple-element.116) | copy-start | bytes 1540
  49.0 34.2 %copy-start.216 = (s32[1024]{0:T(1024)}, s32[1024]{0:T(1024)S(1)}, u32[]{:S(2)}) copy-start(s32[1024]{0:T(1024)S(1)} %pad_clamp_fusion.4) | copy-start | bytes 12292
  52.6 61.8 %copy-start.155 = (f32[4,192]{1,0:T(4,128)}, f32[4,192]{1,0:T(4,128)S(1)}, u32[]{:S(2)}) copy-start(f32[4,192]{1,0:T(4,128)S(1)} %add_divide_fusion.3) | copy-start | bytes 9220
  53.2 134.6 %copy-start.183 = (f32[4,96]{1,0:T(4,128)}, f32[4,96]{1,0:T(4,128)S(1)}, u32[]{:S(2)}) copy-start(f32[4,96]{1,0:T(4,128)S(1)} %get-tuple-element.175) | copy-start | bytes 4612
  54.4 161.8 %copy-start.185 = (f32[4,48]{1,0:T(4,128)}, f32[4,48]{1,0:T(4,128)S(1)}, u32[]{:S(2)}) copy-start(f32[4,48]{1,0:T(4,128)S(1)} %get-tuple-element.172) | copy-start | bytes 2308
  87.8 16.2 %all-to-all-start.1 = ((bf16[4,192,576]{2,1,0:T(8,128)(2,1)}), bf16[4,192,576]{2,1,0:T(8,128)(2,1)S(1)}, u32[]{:S(2)}, u32[]{:S(2)}) async-start(bf16[4,192,576]{2,1,0:T(8,128)(2,1)} %broadcast_select_fusion.3), calls=%async_computation.1 | async-start | bytes 1966080 | tf_op jit(solution)/shard_map/all_to_all | solution.py:381
  131.4 12.3 %all-to-all-start.2 = ((bf16[4,96,576]{2,1,0:T(8,128)(2,1)}), bf16[4,96,576]{2,1,0:T(8,128)(2,1)S(1)}, u32[]{:S(2)}, u32[]{:S(2)}) async-start(bf16[4,96,576]{2,1,0:T(8,128)(2,1)} %copy.204), calls=%async_computation.2 | async-start | bytes 983040 | tf_op jit(solution)/shard_map/all_to_all | solution.py:352
  161.7 14.3 %copy-start.264 = (s32[4]{0:T(128)S(1)}, s32[4]{0:T(128)}, u32[]{:S(2)}) copy-start(s32[4]{0:T(128)} %fusion.300) | copy-start | bytes 52
  163.8 12.1 %all-to-all-start.3 = ((bf16[4,96,576]{2,1,0:T(8,128)(2,1)}), bf16[4,96,576]{2,1,0:T(8,128)(2,1)S(1)}, u32[]{:S(2)}, u32[]{:S(2)}) async-start(bf16[4,96,576]{2,1,0:T(8,128)(2,1)} %broadcast_select_fusion.9), calls=%async_computation.3 | async-start | bytes 983040 | tf_op jit(solution)/shard_map/all_to_all | solution.py:381
  169.7 12.9 %copy-start.232 = (f32[4,96]{1,0:T(4,128)}, f32[4,96]{1,0:T(4,128)S(1)}, u32[]{:S(2)}) copy-start(f32[4,96]{1,0:T(4,128)S(1)} %multiply_reduce_fusion.8) | copy-start | bytes 4612
  169.8 18.1 %copy-start.200 = (f32[4,96]{1,0:T(4,128)}, f32[4,96]{1,0:T(4,128)S(1)}, u32[]{:S(2)}) copy-start(f32[4,96]{1,0:T(4,128)S(1)} %add_divide_fusion.5) | copy-start | bytes 4612
  176.4 11.4 %copy-start.17 = (f32[4,96,576]{2,0,1:T(4,128)}, f32[4,96,576]{2,0,1:T(4,128)S(1)}, u32[]{:S(2)}) copy-start(f32[4,96,576]{2,0,1:T(4,128)S(1)} %fusion.186) | copy-start | bytes 2654212
  176.4 11.4 %slice-start = ((s8[9437184]{0:T(1024)(128)(4,1)}), s8[4194304]{0:T(1024)(128)(4,1)S(1)}, s32[]{:S(2)}) async-start(s8[9437184]{0:T(1024)(128)(4,1)} %bitcast.452), calls=%async_computation.13 | async-start | bytes 8388608
  211.9 10.5 %all-to-all-start.4 = ((bf16[4,48,576]{2,1,0:T(8,128)(2,1)}), bf16[4,48,576]{2,1,0:T(8,128)(2,1)S(1)}, u32[]{:S(2)}, u32[]{:S(2)}) async-start(bf16[4,48,576]{2,1,0:T(8,128)(2,1)} %copy.212), calls=%async_computation.4 | async-start | bytes 491520 | tf_op jit(solution)/shard_map/all_to_all | solution.py:352
  222.4 14.3 %all-to-all-start.6 = ((bf16[4,48,576]{2,1,0:T(8,128)(2,1)}), bf16[4,48,576]{2,1,0:T(8,128)(2,1)}, u32[]{:S(2)}, u32[]{:S(2)}) async-start(bf16[4,48,576]{2,1,0:T(8,128)(2,1)} %copy.221), calls=%async_computation.6 | async-start | bytes 491520 | tf_op jit(solution)/shard_map/all_to_all | solution.py:439
  263.1 13.9 %copy-start.268 = (s32[4]{0:T(128)S(1)}, s32[4]{0:T(128)}, u32[]{:S(2)}) copy-start(s32[4]{0:T(128)} %fusion.302) | copy-start | bytes 52
  264.0 13.3 %copy-start.171 = (s32[4,48]{1,0:T(4,128)S(1)}, s32[4,48]{1,0:T(4,128)}, u32[]{:S(2)}) copy-start(s32[4,48]{1,0:T(4,128)} %copy-done.170) | copy-start | bytes 2308
  264.0 13.3 %copy-start.186 = (f32[4,48]{1,0:T(4,128)S(1)}, f32[4,48]{1,0:T(4,128)}, u32[]{:S(2)}) copy-start(f32[4,48]{1,0:T(4,128)} %copy-done.185) | copy-start | bytes 2308
  264.0 13.3 %copy-start.203 = (f32[4,48]{1,0:T(4,128)S(1)}, f32[4,48]{1,0:T(4,128)}, u32[]{:S(2)}) copy-start(f32[4,48]{1,0:T(4,128)} %copy-done.202) | copy-start | bytes 2308
  264.0 8.5 %all-to-all-start.5 = ((bf16[4,48,576]{2,1,0:T(8,128)(2,1)}), bf16[4,48,576]{2,1,0:T(8,128)(2,1)S(1)}, u32[]{:S(2)}, u32[]{:S(2)}) async-start(bf16[4,48,576]{2,1,0:T(8,128)(2,1)} %get-tuple-element.169), calls=%async_computation.5 | async-start | bytes 491520 | tf_op jit(solution)/shard_map/all_to_all | solution.py:381
  272.5 10.2 %all-to-all-start.7 = ((bf16[4,48,576]{2,1,0:T(8,128)(2,1)}), bf16[4,48,576]{2,1,0:T(8,128)(2,1)S(1)}, u32[]{:S(2)}, u32[]{:S(2)}) async-start(bf16[4,48,576]{2,1,0:T(8,128)(2,1)} %get-tuple-element.168), calls=%async_computation.7 | async-start | bytes 491520 | tf_op jit(solution)/shard_map/all_to_all | solution.py:452
  304.6 11.3 %all-to-all-start.8 = ((bf16[4,96,576]{2,1,0:T(8,128)(2,1)}), bf16[4,96,576]{2,1,0:T(8,128)(2,1)S(1)}, u32[]{:S(2)}, u32[]{:S(2)}) async-start(bf16[4,96,576]{2,1,0:T(8,128)(2,1)} %copy.232), calls=%async_computation.8 | async-start | bytes 983040 | tf_op jit(solution)/shard_map/all_to_all | solution.py:439
  313.6 53.6 %copy-start.199 = (f32[4,96]{1,0:T(4,128)}, f32[4,96]{1,0:T(4,128)S(1)}, u32[]{:S(2)}) copy-start(f32[4,96]{1,0:T(4,128)S(1)} %subtract_multiply_fusion.4) | copy-start | bytes 4612
  342.5 13.1 %all-to-all-start.9 = ((bf16[4,96,576]{2,1,0:T(8,128)(2,1)}), bf16[4,96,576]{2,1,0:T(8,128)(2,1)}, u32[]{:S(2)}, u32[]{:S(2)}) async-start(bf16[4,96,576]{2,1,0:T(8,128)(2,1)} %broadcast_select_fusion.8), calls=%async_computation.9 | async-start | bytes 983040 | tf_op jit(solution)/shard_map/all_to_all | solution.py:452
  387.8 17.3 %all-to-all-start.10 = ((bf16[4,192,576]{2,1,0:T(8,128)(2,1)}), bf16[4,192,576]{2,1,0:T(8,128)(2,1)S(1)}, u32[]{:S(2)}, u32[]{:S(2)}) async-start(bf16[4,192,576]{2,1,0:T(8,128)(2,1)} %copy.243), calls=%async_computation.10 | async-start | bytes 1966080 | tf_op jit(solution)/shard_map/all_to_all | solution.py:439
  392.2 342.3 %all-reduce.4.cloned.1.call-start = ((), (), s32[]{:S(2)}) async-start(), calls=%async_computation.12 | async-start | bytes 29097984 | tf_op jit(solution)/shard_map/psum | solution.py:486
  407.5 12.8 %slice-start.3 = ((s8[9437184]{0:T(1024)(128)(4,1)}), s8[4194304]{0:T(1024)(128)(4,1)S(1)}, s32[]{:S(2)}) async-start(s8[9437184]{0:T(1024)(128)(4,1)} %bitcast.454), calls=%async_computation.16 | async-start | bytes 8388608
  407.5 12.8 %slice-start.4 = ((s8[9437184]{0:T(1024)(128)(4,1)}), s8[4194304]{0:T(1024)(128)(4,1)S(1)}, s32[]{:S(2)}) async-start(s8[9437184]{0:T(1024)(128)(4,1)} %bitcast.454), calls=%async_computation.17 | async-start | bytes 8388608
  473.7 14.3 %copy-start.218 = (f32[4,192]{1,0:T(4,128)S(1)}, f32[4,192]{1,0:T(4,128)}, u32[]{:S(2)}) copy-start(f32[4,192]{1,0:T(4,128)} %copy-done.217) | copy-start | bytes 9220
  473.7 14.3 %copy-start.270 = (s32[4]{0:T(128)S(1)}, s32[4]{0:T(128)}, u32[]{:S(2)}) copy-start(s32[4]{0:T(128)} %copy-done.269) | copy-start | bytes 52
  473.7 14.3 %copy-start.277 = (f32[4,192]{1,0:T(4,128)S(1)}, f32[4,192]{1,0:T(4,128)}, u32[]{:S(2)}) copy-start(f32[4,192]{1,0:T(4,128)} %get-tuple-element.125) | copy-start | bytes 9220
  473.7 14.9 %copy-start.104 = (bf16[576,192]{0,1:T(8,128)(2,1)S(1)}, bf16[576,192]{0,1:T(8,128)(2,1)}, u32[]{:S(2)}) copy-start(bf16[576,192]{0,1:T(8,128)(2,1)} %param.41) | copy-start | bytes 663556
  473.7 14.9 %copy-start.179 = (bf16[3,64,512]{2,1,0:T(8,128)(2,1)S(1)}, bf16[3,64,512]{2,1,0:T(8,128)(2,1)}, u32[]{:S(2)}) copy-start(bf16[3,64,512]{2,1,0:T(8,128)(2,1)} %fusion.119) | copy-start | bytes 589828
  473.7 15.3 %copy-start.110 = (bf16[576,192]{0,1:T(8,128)(2,1)S(1)}, bf16[576,192]{0,1:T(8,128)(2,1)}, u32[]{:S(2)}) copy-start(bf16[576,192]{0,1:T(8,128)(2,1)} %param.40) | copy-start | bytes 663556
  473.7 15.3 %copy-start.137 = (bf16[1,512,3,64]{1,3,2,0:T(8,128)(2,1)S(1)}, bf16[1,512,3,64]{1,3,2,0:T(8,128)(2,1)}, u32[]{:S(2)}) copy-start(bf16[1,512,3,64]{1,3,2,0:T(8,128)(2,1)} %copy-done.136) | copy-start | bytes 589828
  498.6 59.6 %copy-start.262 = (s32[4]{0:T(128)S(1)}, s32[4]{0:T(128)}, u32[]{:S(2)}) copy-start(s32[4]{0:T(128)} %copy-done.259) | copy-start | bytes 52
  498.6 59.6 %all-to-all-start.11 = ((bf16[4,192,576]{2,1,0:T(8,128)(2,1)}), bf16[4,192,576]{2,1,0:T(8,128)(2,1)S(1)}, u32[]{:S(2)}, u32[]{:S(2)}) async-start(bf16[4,192,576]{2,1,0:T(8,128)(2,1)} %broadcast_select_fusion.2), calls=%async_computation.11 | async-start | bytes 1966080 | tf_op jit(solution)/shard_map/all_to_all | solution.py:452
  504.9 54.3 %copy-start.173 = (f32[576]{0:T(1024)S(1)}, f32[576]{0:T(1024)}, u32[]{:S(2)}) copy-start(f32[576]{0:T(1024)} %copy-done.172) | copy-start | bytes 6916
  (262 other events, 862.0 us)
Sparse Core Ops, SparseCore 0:
  470.1 264.3 all-reduce.3
where the time goes:
time: 768 us; the launch traced here: 756 us
  matrix products  290 us (38%)
  waiting for transfers between devices  187 us (24%)
  local copies, waits for them, and re-layouts  98.3 us (13%)
  other arithmetic  57.4 us (7%)
  blocking collectives  53.2 us (7%)
  starting transfers between devices  51.6 us (7%)
  between operations  18.3 us (2%)
    psum x1, waiting for transfers between devices, per_device(): lax.psum((gain_one_total, query_total, key_total, value_total, output_tot...  154 us
    dot_general x18, matrix products, place_rows(): jnp.einsum('sjp,sjd->spd', selector, piece, preferred_element_type=jnp.fl...  121 us
    psum x1, blocking collectives, per_device(): lax.psum((gain_one_total, query_total, key_total, value_total, output_tot...  53.2 us
    dot_general x18, matrix products, pick_rows(): jnp.einsum('sjp,spd->sjd', selector, piece, preferred_element_type=jnp.fl...  53 us
    unnamed x601, local copies, waits for them, and re-layouts  46.9 us
    all_to_all x3, waiting for transfers between devices, per_device(): lax.all_to_all(returned, 'grp', split_axis=0, concat_axis=0, tiled=True)  15.7 us
  transfers between devices with their start and end apart: 13, of which 8 were waited for; matrix products, arithmetic and copies ran while one was open for 17% of the time, Pallas kernels for 0%

commit v1 on v0

--- a/solution.py
+++ b/solution.py
@@ -306,7 +306,6 @@
     routes,
 ):
     seq_count, seq_len, model_width = tokens.shape
-    bucket_count = lax.axis_size("grp")
     own_bucket = lax.axis_index("grp")
     weights = (
         attention_gain.astype(jnp.float32),
@@ -320,109 +319,71 @@
         down_weight,
     )
     router_rows = router.astype(jnp.float32)
-    doc_ends = jnp.cumsum(doc_lengths, axis=-1)
-    source_ids = jnp.arange(bucket_count)
+    lengths = jnp.take(doc_lengths, own_bucket, axis=0)
+    doc_ends = jnp.cumsum(lengths, axis=-1)
+    counts = jnp.take(routes, own_bucket, axis=0)[:, :, 0]
     seq_positions = jnp.arange(seq_len, dtype=jnp.int32)
-    residual = tokens.astype(jnp.float32)
+    picks = [jnp.take(t, own_bucket, axis=0) for t in (picks_first, picks_second, picks_third)]
+    actives = [
+        jnp.arange(p.shape[-1])[None, :] < counts[:, r][:, None] for r, p in enumerate(picks)
+    ]
+    selectors = []
+    for r in range(NREC):
+        outer = jnp.broadcast_to(seq_positions[None], (seq_count, seq_len)) if r == 0 else picks[r - 1]
+        hit = (picks[r][:, :, None] == outer[:, None, :]) & actives[r][:, :, None]
+        if r > 0:
+            hit = hit & actives[r - 1][:, None, :]
+        selectors.append(hit.astype(jnp.bfloat16))
+    touched = jnp.any(selectors[0] > 0, axis=1)
     stored = []
-    for recursion, pick_table in enumerate((picks_first, picks_second, picks_third)):
-        slot_count = pick_table.shape[-1]
-        count_table = routes[:, :, recursion, 0]
-        target_table = routes[:, :, recursion, 1]
-        start_table = jnp.sum(
-            jnp.where(
-                doc_ends[:, :, None, :] <= pick_table[..., None], doc_lengths[:, :, None, :], 0
-            ),
-            axis=-1,
-        )
-        pick_list = jnp.take(pick_table, own_bucket, axis=0)
-        count_list = jnp.take(count_table, own_bucket, axis=0)
-        target_list = jnp.take(target_table, own_bucket, axis=0)
-        active = jnp.arange(slot_count)[None, :] < count_list[:, None]
-        selector = (pick_list[:, :, None] == seq_positions[None, None, :]).astype(jnp.bfloat16)
-        picked_rows = pick_rows(residual, selector)
-        gate_values = jax.nn.sigmoid(jnp.sum(picked_rows * router_rows[recursion], axis=-1))
+    states = []
+    rows_now = jnp.einsum("sjp,spd->sjd", selectors[0], tokens, preferred_element_type=jnp.float32)
+    for r in range(NREC):
+        picked_rows = rows_now
+        active = actives[r]
+        gate_values = jax.nn.sigmoid(jnp.sum(picked_rows * router_rows[r], axis=-1))
         rows_low = picked_rows.astype(jnp.bfloat16)
-        hit_mask = target_list[None, :] == source_ids[:, None]
-        hit_low = hit_mask.astype(jnp.bfloat16)
-        live_rows = jnp.where(active[..., None], rows_low, jnp.zeros((), jnp.bfloat16))
-        outgoing = jnp.einsum(
-            "bs,sjd->bjd", hit_low, live_rows, preferred_element_type=jnp.float32
-        ).astype(jnp.bfloat16)
-        incoming = lax.all_to_all(outgoing, "grp", split_axis=0, concat_axis=0, tiled=True)
-        arriving = target_table == own_bucket
-        arrived = jnp.sum(jnp.where(arriving, count_table, 0), axis=1)
-        source_positions = jnp.sum(jnp.where(arriving[..., None], pick_table, 0), axis=1)
-        source_starts = jnp.sum(jnp.where(arriving[..., None], start_table, 0), axis=1)
-        finish = jnp.cumsum(arrived)
-        first_row = finish - arrived
-        capacity = 2 * (slot_count // 3) * seq_count
-        compact_at = jnp.arange(capacity)
-        source = jnp.sum((finish[None, :] <= compact_at[:, None]).astype(jnp.int32), axis=1)
-        source_first = jnp.sum(
-            jnp.where(source_ids[None, :] == source[:, None], first_row[None, :], 0), axis=1
-        )
-        flat_index = source * slot_count + compact_at - source_first
-        packed = jnp.take(
-            incoming.reshape(bucket_count * slot_count, model_width), flat_index, axis=0
-        )[None]
-        positions = jnp.take(source_positions.reshape(-1), flat_index)[None]
-        doc_start = jnp.take(source_starts.reshape(-1), flat_index)[None]
-        allowed = attention_mask(
-            source[None], doc_start, positions, jnp.ones((1, capacity), dtype=bool)
-        )
-        change, log_total = block_forward(packed, allowed, positions, weights)
-        slot_index = jnp.clip(first_row[:, None] + jnp.arange(slot_count)[None, :], 0, capacity - 1)
-        slot_live = jnp.arange(slot_count)[None, :] < arrived[:, None]
-        change_slots = jnp.take(
-            change.astype(jnp.bfloat16), slot_index.reshape(-1), axis=0
-        ).reshape(bucket_count, slot_count, model_width)
-        returned = jnp.where(slot_live[..., None], change_slots, jnp.zeros((), jnp.bfloat16))
-        coming_back = lax.all_to_all(returned, "grp", split_axis=0, concat_axis=0, tiled=True)
-        change_rows = jnp.einsum(
-            "bs,bjd->sjd", hit_low, coming_back, preferred_element_type=jnp.float32
-        )
-        stored.append(
-            (
-                selector,
-                active,
-                picked_rows,
-                gate_values,
-                change_rows,
-                hit_low,
-                packed,
-                allowed,
-                positions,
-                log_total,
-                flat_index,
-                slot_index,
-                slot_live,
+        starts = jnp.sum(
+            jnp.where(doc_ends[:, None, :] <= picks[r][..., None], lengths[:, None, :], 0), axis=-1
+        )
+        allowed = attention_mask(jnp.zeros_like(picks[r]), starts, picks[r], active)
+        change, log_total = block_forward(rows_low, allowed, picks[r], weights)
+        change_rows = change.astype(jnp.bfloat16).astype(jnp.float32).reshape(picked_rows.shape)
+        stored.append((picked_rows, gate_values, rows_low, allowed, change_rows, log_total))
+        update = gate_values[..., None] * change_rows * active[..., None].astype(jnp.float32)
+        states.append(picked_rows + update)
+        if r + 1 < NREC:
+            rows_now = pick_rows(states[r], selectors[r + 1])
+    final = states[-1]
+    for r in (1, 0):
+        inside = jnp.any(selectors[r + 1] > 0, axis=1)
+        parts = exact_parts(final)
+        spread = sum(
+            jnp.einsum("sjp,sjd->spd", selectors[r + 1], part, preferred_element_type=jnp.float32)
+            for part in parts
+        )
+        final = jnp.where(inside[..., None], spread, states[r])
+    placed = jnp.einsum(
+        "sjp,sjd->spd", selectors[0], final.astype(jnp.bfloat16), preferred_element_type=jnp.float32
+    ).astype(jnp.bfloat16)
+    out_state = jnp.where(touched[..., None], placed, tokens)
+
+    grads = [jnp.einsum("sjp,spd->sjd", selectors[0], out_grad, preferred_element_type=jnp.float32)]
+    for r in (1, 2):
+        grads.append(
+            jnp.einsum(
+                "sjp,spd->sjd",
+                selectors[r],
+                grads[-1].astype(jnp.bfloat16),
+                preferred_element_type=jnp.float32,
             )
         )
-        update = gate_values[..., None] * change_rows * active[..., None].astype(jnp.float32)
-        residual = place_rows(residual, selector, update)
     grad_totals = tuple((jnp.zeros(weight_item.shape, jnp.float32) for weight_item in weights))
     router_terms = [None] * NREC
-    residual_grad = out_grad.astype(jnp.float32)
-    for recursion in (2, 1, 0):
-        (
-            selector,
-            active,
-            picked_rows,
-            gate_values,
-            change_rows,
-            hit_low,
-            packed,
-            allowed,
-            positions,
-            log_total,
-            flat_index,
-            slot_index,
-            slot_live,
-        ) = stored[recursion]
-        slot_count = selector.shape[1]
-        active_float = active.astype(jnp.float32)
-        row_grad = pick_rows(residual_grad, selector)
+    for r in (2, 1, 0):
+        picked_rows, gate_values, rows_low, allowed, change_rows, log_total = stored[r]
+        row_grad = grads[r]
+        active_float = actives[r].astype(jnp.float32)
         change_grad = (gate_values[..., None] * row_grad * active_float[..., None]).astype(
             jnp.bfloat16
         )
@@ -432,86 +393,27 @@
             * gate_values
             * (1.0 - gate_values)
         )
-        router_terms[recursion] = jnp.sum(logit_grad[..., None] * picked_rows, axis=(0, 1))
-        outgoing_grad = jnp.einsum(
-            "bs,sjd->bjd", hit_low, change_grad, preferred_element_type=jnp.float32
-        ).astype(jnp.bfloat16)
-        incoming_grad = lax.all_to_all(
-            outgoing_grad, "grp", split_axis=0, concat_axis=0, tiled=True
-        )
-        packed_grad = jnp.take(
-            incoming_grad.reshape(bucket_count * slot_count, model_width), flat_index, axis=0
-        )[None]
+        router_terms[r] = jnp.sum(logit_grad[..., None] * picked_rows, axis=(0, 1))
         rows_grad, grad_terms = block_backward(
-            packed, allowed, positions, log_total, packed_grad, weights
-        )
-        grad_slots = jnp.take(
-            rows_grad.astype(jnp.bfloat16), slot_index.reshape(-1), axis=0
-        ).reshape(bucket_count, slot_count, model_width)
-        back_slots = jnp.where(slot_live[..., None], grad_slots, jnp.zeros((), jnp.bfloat16))
-        coming_grad = lax.all_to_all(back_slots, "grp", split_axis=0, concat_axis=0, tiled=True)
-        sent_grad = jnp.einsum(
-            "bs,bjd->sjd", hit_low, coming_grad, preferred_element_type=jnp.float32
+            rows_low, allowed, picks[r], log_total, change_grad, weights
         )
         grad_totals = tuple(
             (running + fresh_term for running, fresh_term in zip(grad_totals, grad_terms))
         )
-        total_grad = (logit_grad[..., None] * router_rows[recursion] + sent_grad) * active_float[
-            ..., None
-        ]
-        residual_grad = place_rows(residual_grad, selector, total_grad)
+        sent_grad = rows_grad.astype(jnp.bfloat16).astype(jnp.float32).reshape(row_grad.shape)
+        total = (logit_grad[..., None] * router_rows[r] + sent_grad) * active_float[..., None]
+        grads[r] = row_grad + total
+        extra = total if r == 2 else extra + total
+        if r > 0:
+            extra = place_rows(jnp.zeros_like(grads[r - 1]), selectors[r], extra)
+            grads[r - 1] = grads[r - 1] + extra
+    placed_grad = jnp.einsum(
+        "sjp,sjd->spd", selectors[0], grads[0].astype(jnp.bfloat16), preferred_element_type=jnp.float32
+    ).astype(jnp.bfloat16)
+    grad_tokens = jnp.where(touched[..., None], placed_grad, out_grad)
     router_grad = jnp.stack(router_terms, 0)
-    (
-        gain_one_total,
-        query_total,
-        key_total,
-        value_total,
-        output_total,
-        gain_two_total,
-        gate_total,
-        up_total,
-        down_total,
-    ) = grad_totals
-    (
-        gain_one_sum,
-        query_sum,
-        key_sum,
-        value_sum,
-        output_sum,
-        gain_two_sum,
-        gate_sum,
-        up_sum,
-        down_sum,
-        router_sum,
-    ) = lax.psum(
-        (
-            gain_one_total,
-            query_total,
-            key_total,
-            value_total,
-            output_total,
-            gain_two_total,
-            gate_total,
-            up_total,
-            down_total,
-            router_grad,
-        ),
-        ("grp", "rep"),
-    )
-    return (
-        residual.astype(jnp.bfloat16),
-        residual_grad.astype(jnp.bfloat16),
-        gain_one_sum,
-        query_sum,
-        key_sum,
-        value_sum,
-        output_sum,
-        gain_two_sum,
-        gate_sum,
-        up_sum,
-        down_sum,
-        router_sum,
-    )
+    sums = lax.psum(grad_totals + (router_grad,), ("grp", "rep"))
+    return (out_state, grad_tokens) + tuple(sums)
 
 
 def solution(mesh):

time: 768 us -> 628 us (0.82)
  matrix products: 290 us -> 199 us
  starting transfers between devices: 51.6 us -> 0.04 us
  local copies, waits for them, and re-layouts: 98.3 us -> 109 us
  blocking collectives: 53.2 us -> 44 us
    dot_general x18 -> x6, matrix products: 121 us -> 7.62 us  [place_rows(): jnp.einsum('sjp,sjd->spd', selector, piece, preferred_element_type=jnp.fl...]
    all_to_all x12 -> x0, starting transfers between devices: 51.6 us -> none  [the longest x3 14.2 us: per_device(): lax.all_to_all(back_slots, 'grp', split_axis=0, concat_axis=0, tiled=True)]
    dot_general x18 -> x6, matrix products: 53 us -> 4.86 us  [pick_rows(): jnp.einsum('sjp,spd->sjd', selector, piece, preferred_element_type=jnp.fl...]
    gather x24 -> x0, local copies, waits for them, and re-layouts: 41.1 us -> none  [the longest x6 8.89 us: per_device(): jnp.take(incoming.reshape(bucket_count * slot_count, model_width), flat_i...]
    reshape x6 -> x21, local copies, waits for them, and re-layouts: 0.49 us -> 40.7 us  [the longest x3 7.28 us: block_backward(): mixed_grad.reshape(group_count, length, kv_count, per_group, HEAD_DIM)]
    all_to_all x12 -> x0, waiting for transfers between devices: 33.1 us -> none  [the longest x3 15.7 us: per_device(): lax.all_to_all(returned, 'grp', split_axis=0, concat_axis=0, tiled=True)]
    psum x1, waiting for transfers between devices: 154 us -> 186 us  [per_device(): sums = lax.psum(grad_totals + (router_grad,), ('grp', 'rep'))]
    dot_general x12 -> x11, matrix products: 8.6 us -> 29.8 us  [the longest x1 7.95 us: per_device(): jnp.einsum('sjp,sjd->spd', selectors[0], final.astype(jnp.bfloat16), pref...]
  transfers between devices with their start and end apart: 13 -> 1, of which waited for: 8 -> 1; matrix products, arithmetic and copies ran while one was open for 17% -> 5% of each run, Pallas kernels for 0% -> 0%
where the time goes in v1:
time: 628 us; the launch traced here: 620 us
  matrix products  199 us (32%)
  waiting for transfers between devices  186 us (30%)
  local copies, waits for them, and re-layouts  109 us (17%)
  other arithmetic  63.9 us (10%)
  blocking collectives  44 us (7%)
  between operations  17.6 us (3%)
    psum x1, waiting for transfers between devices, per_device(): sums = lax.psum(grad_totals + (router_grad,), ('grp', 'rep'))  186 us
    psum x1, blocking collectives, per_device(): sums = lax.psum(grad_totals + (router_grad,), ('grp', 'rep'))  44 us
    unnamed x558, local copies, waits for them, and re-layouts  40.3 us
  transfers between devices with their start and end apart: 1, of which 1 were waited for; matrix products, arithmetic and copies ran while one was open for 5% of the time, Pallas kernels for 0%

profile of v1, /device:TPU:1, one launch (start us, length us, event | category | flops | bytes accessed | tf_op | source)
XLA Modules:
  0.0 620.2 jit_solution(6725950436511125619)
XLA Ops:
  14.2 5.8 multiply_reduce_fusion.3
  20.8 3.1 multiply_convert_fusion.7
  30.9 2.6 fusion.20
  41.2 2.5 convolution_convert_fusion.5
  45.8 4.8 fusion.35
  52.6 3.4 convert_element_type.516
  56.0 2.4 multiply_reduce_fusion.8
  62.6 4.9 multiply_convert_fusion.2
  74.6 2.4 multiply_add_fusion
  93.5 2.3 convert_element_type.540
  95.8 2.3 multiply_reduce_fusion.18
  100.9 2.7 multiply_convert_fusion.5
  106.7 2.4 copy.135
  137.2 2.5 bitcast_add_fusion
  142.2 3.7 fusion.8
  177.1 2.3 reshape.865
  185.3 2.2 multiply_reduce_fusion.10
  189.5 4.1 multiply_convert_fusion.3
  201.2 2.3 reshape.871
  213.6 2.2 fusion.192
  220.8 3.2 multiply_reduce_fusion.14
  225.5 2.5 copy.157
  228.1 2.4 multiply_reduce_fusion.9
  232.4 2.6 fusion.205
  235.0 2.5 fusion.203
  237.4 2.4 fusion.201
  243.3 2.9 multiply_reduce_fusion.1
  246.2 3.4 fusion.206
  249.6 4.4 multiply_convert_fusion
  254.0 3.3 fusion.202
  257.3 2.8 fusion.194
  263.8 5.1 fusion.204
  269.0 2.5 multiply_reduce_fusion.4
  275.4 2.9 reshape.878
  278.3 4.9 fusion.57
  283.3 4.8 fusion
  289.9 2.4 fusion.2
  294.5 2.9 bitcast_multiply_fusion.1
  312.3 2.7 reshape.879
  315.0 6.5 %add_add_fusion = f32[1536,576]{0,1:T(8,128)} fusion(f32[1536,576]{0,1:T(8,128)} %fusion.206, f32[1536,576]{0,1:T(8,128)} %fusion.205, bf16[384,1536]{1,0:T(8,128)(2,1)} %copy-done.149, bf16[384,576]{1,0:T(8,128)(2,1)S(1)} %bitcast.385), kind=kOutput, calls=%fused_computation.16 | convolution fusion | flops 681246720 | bytes 12238848 | tf_op jit(solution)/shard_map/rf,rd->fd/dot_general | solution.py:203
  321.5 2.9 add_add_fusion.1
  326.1 2.9 add_add_fusion.2
  344.1 3.3 copy.168
  347.5 44.0 %all-reduce = (f32[576]{0:T(1024)}, f32[576]{0:T(1024)}, f32[3,576]{1,0:T(4,128)}) all-reduce(f32[576]{0:T(1024)S(1)} %add_add_fusion.8, f32[576]{0:T(1024)S(1)} %add_add_fusion.7, f32[3,576]{1,0:T(4,128)S(1)} %pad_maximum_fusion.6), channel_id=1, replica_groups=mesh['grp'=4,'rep'=8] {'grp','rep'}, use_global_device_ids=true, to_apply=%region_37.38 | all-reduce | flops 2880 | bytes 23040 | tf_op jit(solution)/shard_map/psum | solution.py:415
  398.6 5.5 convert_select_fusion
  404.1 7.9 %convert_select_fusion.1 = bf16[4,1024,576]{1,2,0:T(8,128)(2,1)} fusion(bf16[4,1024,576]{1,2,0:T(8,128)(2,1)} %param.17, pred[4,1024]{1,0:T(4,128)(4,1)S(1)} %compare_reduce_fusion, s32[4,192]{1,0:T(4,128)S(1)} %get-tuple-element.110, pred[4,192]{1,0:T(4,128)(4,1)S(1)} %copy-done.186, f32[4,192,576]{2,1,0:T(8,128)} %copy-done.3, ...), kind=kOutput, calls=%fused_computation.12 | convolution fusion | flops 1000292352 | bytes 15640960 | tf_op jit(solution)/shard_map/sjp,sjd->spd/dot_general | solution.py:366
  412.0 186.2 %all-reduce.4.cloned.1.call-done = (f32[576,576]{1,0:T(8,128)}, f32[576,192]{0,1:T(8,128)}, f32[576,192]{0,1:T(8,128)}, f32[576,576]{1,0:T(8,128)}, f32[576,1536...) async-done(((f32[576,576]{1,0:T(8,128)}, f32[576,192]{0,1:T(8,128)}, f32[576,192]{0,1:T(8,128)}, f32[576,576]{1,0:T(8,128)}, f32[576,1536]{1,0:T(8,128)}, ...) | async-done | bytes 14155792 | tf_op jit(solution)/shard_map/psum | solution.py:415
  598.3 2.7 copy.259
  (773 shorter events, 219.1 us)
Async XLA Ops:
  7.2 61.7 %copy-start = (bf16[1536,576]{0,1:T(8,128)(2,1)S(1)}, bf16[1536,576]{0,1:T(8,128)(2,1)}, u32[]{:S(2)}) copy-start(bf16[1536,576]{0,1:T(8,128)(2,1)} %param.26) | copy-start | bytes 5308420
  7.2 591.1 %all-reduce.4.cloned.1.call-start = ((), (), s32[]{:S(2)}) async-start(), calls=%async_computation | async-start | bytes 29097984 | tf_op jit(solution)/shard_map/psum | solution.py:415
  10.1 23.6 %copy-start.182 = (pred[4,192]{1,0:T(4,128)(4,1)}, pred[4,192]{1,0:T(4,128)(4,1)S(1)}, u32[]{:S(2)}) copy-start(pred[4,192]{1,0:T(4,128)(4,1)S(1)} %get-tuple-element.178) | copy-start | bytes 2308
  12.1 8.0 %copy-start.258 = (f32[576]{0:T(1024)}, f32[576]{0:T(1024)S(1)}, u32[]{:S(2)}) copy-start(f32[576]{0:T(1024)S(1)} %get-tuple-element.85) | copy-start | bytes 6916
  14.2 9.6 %copy-start.75 = (bf16[576,576]{0,1:T(8,128)(2,1)}, bf16[576,576]{0,1:T(8,128)(2,1)S(1)}, u32[]{:S(2)}) copy-start(bf16[576,576]{0,1:T(8,128)(2,1)S(1)} %copy.121) | copy-start | bytes 1990660
  20.8 20.4 %copy-start.197 = (f32[768]{0:T(1024)}, f32[768]{0:T(1024)S(1)}, u32[]{:S(2)}) copy-start(f32[768]{0:T(1024)S(1)} %rsqrt.67) | copy-start | bytes 9220
  28.4 5.1 copy-start.204
  28.6 4.9 copy-start.217
  41.2 14.7 %copy-start.4 = (f32[768,576]{0,1:T(8,128)}, f32[768,576]{0,1:T(8,128)S(1)}, u32[]{:S(2)}) copy-start(f32[768,576]{0,1:T(8,128)S(1)} %copy.120) | copy-start | bytes 5308420
  62.6 4.9 copy-start.266
  73.4 5.0 copy-start.175
  109.1 4.9 copy-start.177
  112.4 7.0 %copy-start.170 = (s32[4,48]{1,0:T(4,128)}, s32[4,48]{1,0:T(4,128)S(1)}, u32[]{:S(2)}) copy-start(s32[4,48]{1,0:T(4,128)S(1)} %get-tuple-element.100) | copy-start | bytes 2308
  139.8 13.1 %copy-start.21 = (f32[192,576]{1,0:T(8,128)}, f32[192,576]{1,0:T(8,128)S(1)}, u32[]{:S(2)}) copy-start(f32[192,576]{1,0:T(8,128)S(1)} %get-tuple-element.196) | copy-start | bytes 1327108
  139.9 12.9 %copy-start.225 = (f32[192]{0:T(256)}, f32[192]{0:T(256)S(1)}, u32[]{:S(2)}) copy-start(f32[192]{0:T(256)S(1)} %add_rsqrt_fusion.5) | copy-start | bytes 2308
  211.6 9.2 %copy-start.17 = (f32[384,576]{0,1:T(8,128)S(1)}, f32[384,576]{0,1:T(8,128)}, u32[]{:S(2)}) copy-start(f32[384,576]{0,1:T(8,128)} %copy-done.16) | copy-start | bytes 2654212
  211.6 9.2 %copy-start.35 = (bf16[576,576]{1,0:T(8,128)(2,1)S(1)}, bf16[576,576]{1,0:T(8,128)(2,1)}, u32[]{:S(2)}) copy-start(bf16[576,576]{1,0:T(8,128)(2,1)} %param.19) | copy-start | bytes 1990660
  235.0 14.6 %slice-start.4 = ((s8[4718592]{0:T(1024)(128)(4,1)}), s8[4194304]{0:T(1024)(128)(4,1)S(1)}, s32[]{:S(2)}) async-start(s8[4718592]{0:T(1024)(128)(4,1)} %bitcast.406), calls=%async_computation.5 | async-start | bytes 8388608
  239.9 9.6 %slice-start.2 = ((s8[4718592]{0:T(1024)(128)(4,1)}), s8[4194304]{0:T(1024)(128)(4,1)S(1)}, s32[]{:S(2)}) async-start(s8[4718592]{0:T(1024)(128)(4,1)} %bitcast.404), calls=%async_computation.3 | async-start | bytes 8388608
  243.3 6.3 %slice-start.3 = ((s8[4718592]{0:T(1024)(128)(4,1)}), s8[524288]{0:T(1024)(128)(4,1)S(1)}, s32[]{:S(2)}) async-start(s8[4718592]{0:T(1024)(128)(4,1)} %bitcast.404), calls=%async_computation.4 | async-start | bytes 1048576
  243.3 6.3 %slice-start.5 = ((s8[4718592]{0:T(1024)(128)(4,1)}), s8[524288]{0:T(1024)(128)(4,1)S(1)}, s32[]{:S(2)}) async-start(s8[4718592]{0:T(1024)(128)(4,1)} %bitcast.406), calls=%async_computation.6 | async-start | bytes 1048576
  263.7 5.2 copy-start.9
  263.7 5.2 copy-start.65
  263.8 5.2 copy-start.200
  263.8 5.2 copy-start.264
  263.8 5.2 copy-start.265
  273.7 4.6 copy-start.167
  278.3 5.0 copy-start.74
  278.3 5.0 copy-start.113
  278.3 11.6 %slice-start = ((s8[7077888]{0:T(1024)(128)(4,1)}), s8[4194304]{0:T(1024)(128)(4,1)S(1)}, s32[]{:S(2)}) async-start(s8[7077888]{0:T(1024)(128)(4,1)} %bitcast.357), calls=%async_computation.1 | async-start | bytes 8388608
  283.3 4.8 copy-start.97
  283.3 6.6 %slice-start.1 = ((s8[7077888]{0:T(1024)(128)(4,1)}), s8[2883584]{0:T(1024)(128)(4,1)S(1)}, s32[]{:S(2)}) async-start(s8[7077888]{0:T(1024)(128)(4,1)} %bitcast.357), calls=%async_computation.2 | async-start | bytes 5767168
  297.4 5.1 copy-start.163
  301.1 4.7 copy-start.120
  310.4 4.6 copy-start.93
  315.0 6.5 %copy-start.11 = (f32[576,1536]{1,0:T(8,128)S(1)}, f32[576,1536]{1,0:T(8,128)}, u32[]{:S(2)}) copy-start(f32[576,1536]{1,0:T(8,128)} %fusion.203) | copy-start | bytes 10616836
  315.0 6.5 %copy-start.99 = (bf16[384,576]{0,1:T(8,128)(2,1)S(1)}, bf16[384,576]{0,1:T(8,128)(2,1)}, u32[]{:S(2)}) copy-start(bf16[384,576]{0,1:T(8,128)(2,1)} %copy-done.98) | copy-start | bytes 1327108
  315.0 6.5 %copy-start.104 = (f32[576,1536]{1,0:T(8,128)S(1)}, f32[576,1536]{1,0:T(8,128)}, u32[]{:S(2)}) copy-start(f32[576,1536]{1,0:T(8,128)} %fusion.204) | copy-start | bytes 10616836
  315.0 6.5 %copy-start.153 = (bf16[384,1536]{1,0:T(8,128)(2,1)S(1)}, bf16[384,1536]{1,0:T(8,128)(2,1)}, u32[]{:S(2)}) copy-start(bf16[384,1536]{1,0:T(8,128)(2,1)} %copy-done.152) | copy-start | bytes 3538948
  321.5 4.6 copy-start.151
  344.0 47.5 %copy-start.174 = (s32[4,48]{1,0:T(4,128)S(1)}, s32[4,48]{1,0:T(4,128)}, u32[]{:S(2)}) copy-start(s32[4,48]{1,0:T(4,128)} %copy-done.170) | copy-start | bytes 2308
  344.0 47.4 %copy-start.181 = (pred[4,96]{1,0:T(4,128)(4,1)S(1)}, pred[4,96]{1,0:T(4,128)(4,1)}, u32[]{:S(2)}) copy-start(pred[4,96]{1,0:T(4,128)(4,1)} %copy-done.175) | copy-start | bytes 1156
  344.0 47.4 %copy-start.196 = (pred[4,48]{1,0:T(4,128)(4,1)S(1)}, pred[4,48]{1,0:T(4,128)(4,1)}, u32[]{:S(2)}) copy-start(pred[4,48]{1,0:T(4,128)(4,1)} %copy-done.192) | copy-start | bytes 580
  344.0 47.6 %copy-start.186 = (pred[4,192]{1,0:T(4,128)(4,1)S(1)}, pred[4,192]{1,0:T(4,128)(4,1)}, u32[]{:S(2)}) copy-start(pred[4,192]{1,0:T(4,128)(4,1)} %copy-done.182) | copy-start | bytes 2308
  344.0 49.0 %copy-start.79 = (bf16[192,576]{1,0:T(8,128)(2,1)S(1)}, bf16[192,576]{1,0:T(8,128)(2,1)}, u32[]{:S(2)}) copy-start(bf16[192,576]{1,0:T(8,128)(2,1)} %copy-done.78) | copy-start | bytes 663556
  344.1 49.0 %copy-start.189 = (f32[4,48]{1,0:T(4,128)S(1)}, f32[4,48]{1,0:T(4,128)}, u32[]{:S(2)}) copy-start(f32[4,48]{1,0:T(4,128)} %get-tuple-element.173) | copy-start | bytes 2308
  344.1 49.0 %copy-start.203 = (f32[4,48]{1,0:T(4,128)S(1)}, f32[4,48]{1,0:T(4,128)}, u32[]{:S(2)}) copy-start(f32[4,48]{1,0:T(4,128)} %copy-done.202) | copy-start | bytes 2308
  607.8 5.1 copy-start.1
  (228 other events, 512.0 us)
Sparse Core Ops, SparseCore 0:
  336.0 262.2 all-reduce.3
